TPU v7x, 32 devices: a whole 2x2x4 slice. The times are simulated.
32 devices in a mesh: group: 4 (over x, core), seq: 8 (over z, y).
Axes of the slice: x: 2, y: 2, z: 4, core: 2. Of those that a mesh axis runs over, the one named last changes fastest.
Arguments:
- features: bfloat16 [16, 64, 16, 384], P('group', 'seq'), parts along dimension 0, may hold values from -6 to 6
- cotangent: bfloat16 [16, 64, 16, 192], P('group', 'seq'), parts along dimension 0, may hold values from -6 to 6
- conv_weight: bfloat16 [3, 3, 3, 384, 192], replicated, may hold values from -0.0625 to 0.0625
- patch_map: bfloat16 [1536, 4096], P('seq'), may hold values from -0.15625 to 0.15625
- qkv: bfloat16 [3, 4096, 4096], P(None, ('group', 'seq')), parts along dimension 1, may hold values from -122 to 122
Outputs:
- weight_grad: float32 [12, 3, 3, 384, 192], P('group'), parts along dimension 0
- grad_qkv: bfloat16 [3, 4096, 4096], P(None, ('group', 'seq')), parts along dimension 1
There are 4 independent parts, one for each index of `group`. A program takes and returns all parts, laid end to end along the dimension named above; an argument that names none is the same for every part. Nothing has to cross between parts.
All inputs are finite; a program needn't handle non-finite values.
Results may differ from a plain program's by a relative error of at most 0.0075.
Values may be sent and summed in bfloat16 or wider, within the bound.
A program may use at most 128 MiB of HBM per device.

v0:
```python
import math

import jax
import jax.numpy as jnp
from jax import lax
from jax.experimental import pallas as pl
from jax.experimental.pallas import tpu as pltpu
from jax.sharding import PartitionSpec as P

HEADS = 32
TILE = 32
LIMIT = 60 * 1024 * 1024


def flops(count, moved):
    return pl.CostEstimate(flops=count, bytes_accessed=moved, transcendentals=0)


def grad_out_kernel(x_ref, w_ref, map_ref, out_ref, acc_ref):
    frames, span, wide = x_ref.shape[1], x_ref.shape[2], x_ref.shape[3]
    double = w_ref.shape[2]
    tap_h = pl.program_id(1)

    for side in range(2):
        for tap_t in (2, 1, 0):
            live = frames - 2 + tap_t
            rows = x_ref[side + 2 - tap_h, 2 - tap_t :].reshape(live * span, wide)
            part = lax.dot_general(
                rows, w_ref[tap_t, 0], (((1,), (1,)), ((), ())), preferred_element_type=jnp.float32
            )
            if tap_t == 2:

                @pl.when(tap_h == 0)
                def _():
                    acc_ref[side] = part

                @pl.when(tap_h > 0)
                def _():
                    acc_ref[side] += part

            else:
                acc_ref[side, : live * span] += part

    @pl.when(tap_h == 2)
    def _():
        wide_out = out_ref.shape[1]
        total = jnp.dot(
            acc_ref[0].astype(jnp.bfloat16), map_ref[:double], preferred_element_type=jnp.float32
        ) + jnp.dot(
            acc_ref[1].astype(jnp.bfloat16), map_ref[double:], preferred_element_type=jnp.float32
        )
        each = span // TILE
        total = total.reshape(frames, TILE, each, wide_out).transpose(1, 0, 2, 3)
        out_ref[...] = total.reshape(frames * span, wide_out).astype(jnp.bfloat16)


def weight_kernel(scale, blocks, feat_ref, x_ref, out_ref, turned_ref):
    frames, span, wide = x_ref.shape[1], x_ref.shape[2], x_ref.shape[3]
    double = feat_ref.shape[4]
    cin, cout = double // 2, wide // 4
    tap_h = pl.program_id(0)
    block = pl.program_id(1)

    def turn():
        for side in range(2):
            for frame in range(frames):
                turned_ref[side, :, frame * span : (frame + 1) * span] = (
                    feat_ref[:, side, frame].reshape(span, double).T
                )

    if blocks == 1:
        pl.when(tap_h == 0)(turn)
    else:
        turn()
    for tap_t in range(3):
        live = frames - 2 + tap_t
        prod = None
        for side in range(2):
            rows = x_ref[side + 2 - tap_h, 2 - tap_t :].reshape(live * span, wide)
            part = jnp.dot(
                turned_ref[side, :, : live * span], rows, preferred_element_type=jnp.float32
            )
            prod = part if prod is None else prod + part
        for tap_w in range(3):
            even = prod[:cin, cout * (2 - tap_w) : cout * (3 - tap_w)]
            odd = prod[cin:, cout * (3 - tap_w) : cout * (4 - tap_w)]
            value = (even + odd) * scale
            if blocks == 1:
                out_ref[tap_t, 0, tap_w] = value
            else:

                @pl.when(block == 0)
                def _():
                    out_ref[tap_t, 0, tap_w] = value

                @pl.when(block > 0)
                def _():
                    out_ref[tap_t, 0, tap_w] += value


def attention_kernel(step, qkv_ref, grad_ref, out_ref, dk_ref, dv_ref):
    shards, _, rows, width = qkv_ref.shape
    length = shards * rows
    scale = 1.0 / math.sqrt(width)
    keys = qkv_ref[:, 1].reshape(length, width)
    values = qkv_ref[:, 2].reshape(length, width)
    keys_t = keys.T
    span = step * rows

    def block(index, first):
        query = qkv_ref[pl.ds(index * step, step), 0].reshape(span, width)
        grads = grad_ref[pl.ds(pl.multiple_of(index * span, span), span), :]
        scores = lax.dot_general(
            keys, query, (((1,), (1,)), ((), ())), preferred_element_type=jnp.float32
        )
        top = jnp.max(scores, axis=0, keepdims=True)
        expo = jnp.exp((scores - top) * scale)
        probs = expo * (1.0 / jnp.sum(expo, axis=0, keepdims=True))
        dprob = lax.dot_general(
            values, grads, (((1,), (1,)), ((), ())), preferred_element_type=jnp.float32
        )
        delta = jnp.sum(probs * dprob, axis=0, keepdims=True)
        dscore = (probs * (dprob - delta)).astype(jnp.bfloat16)
        dquery = jnp.dot(keys_t, dscore, preferred_element_type=jnp.float32) * scale
        out_ref[pl.ds(index * step, step), 0] = (
            dquery.T.reshape(step, rows, width).astype(jnp.bfloat16)
        )
        part_k = jnp.dot(dscore, query, preferred_element_type=jnp.float32)
        part_v = jnp.dot(probs.astype(jnp.bfloat16), grads, preferred_element_type=jnp.float32)
        if first:
            dk_ref[...] = part_k
            dv_ref[...] = part_v
        else:
            dk_ref[...] += part_k
            dv_ref[...] += part_v

    count = shards // step
    if count <= 4:
        for index in range(count):
            block(index, index == 0)
    else:
        block(0, True)

        @pl.loop(1, count)
        def _(index):
            block(index, False)

    out_ref[:, 1] = (dk_ref[...] * scale).reshape(shards, rows, width).astype(jnp.bfloat16)
    out_ref[:, 2] = dv_ref[...].reshape(shards, rows, width).astype(jnp.bfloat16)


def per_device(features, cotangent, conv_weight, patch_map, qkv):
    frames, rows_here, cols, cin = features.shape
    cout = cotangent.shape[3]
    count = lax.axis_size("seq")
    parts = lax.axis_size("group")
    half, pairs = cols // 2, rows_here // 2
    pairs_all = pairs * count
    tokens_here, inner = qkv.shape[1], qkv.shape[2]
    length = tokens_here * count
    mine = inner // count
    head_dim = inner // HEADS

    cot = cotangent.reshape(frames, pairs, 2, half, 2 * cout).transpose(2, 0, 1, 3, 4)
    cot = lax.all_gather(cot.reshape(-1, 2 * cout), "seq", axis=0, tiled=True)
    sent = qkv.reshape(3, tokens_here, count, mine).transpose(2, 0, 1, 3)
    moved = lax.all_to_all(sent, "seq", split_axis=0, concat_axis=0, tiled=True)
    share = mine // parts
    depth = patch_map.shape[0]
    member = lax.axis_index("group")
    piece = lax.dynamic_index_in_dim(
        patch_map.reshape(depth, count, parts, share), member, axis=2, keepdims=False
    )
    piece = lax.all_to_all(
        piece.transpose(1, 0, 2), "seq", split_axis=0, concat_axis=0, tiled=True
    ).reshape(count * depth, share)
    columns = lax.all_gather(piece, "group", axis=0, tiled=False)
    columns = columns.transpose(1, 0, 2).reshape(count * depth, mine)
    feat = features.reshape(frames, pairs, 2, half, 2 * cin).transpose(2, 0, 1, 3, 4)
    feat = lax.all_gather(feat.reshape(-1, 2 * cin), "seq", axis=0, tiled=True)
    feat = feat.reshape(count, 2, frames, pairs * half, 2 * cin)

    full = cot.reshape(count, 2, frames, pairs, half, 2 * cout).transpose(1, 2, 0, 3, 4, 5)
    full = full.reshape(2, frames, pairs_all, half, 2 * cout)
    left = jnp.pad(full[:, :, :, :-1, cout:], ((0, 0), (0, 0), (0, 0), (1, 0), (0, 0)))
    right = jnp.pad(full[:, :, :, 1:, :cout], ((0, 0), (0, 0), (0, 0), (0, 1), (0, 0)))
    wide = jnp.concatenate([left, full, right], axis=-1)
    above = jnp.pad(wide[1][:, :-1], ((0, 0), (1, 0), (0, 0), (0, 0)))
    below = jnp.pad(wide[0][:, 1:], ((0, 0), (0, 1), (0, 0), (0, 0)))
    shifts = jnp.stack([above, wide[0], wide[1], below])
    shifts = shifts.reshape(4, frames, pairs_all * half, 4 * cout)

    taps = [conv_weight[:, :, tap_w] for tap_w in range(3)]
    blank = jnp.zeros_like(taps[0])
    big = jnp.concatenate(
        [
            jnp.concatenate([taps[2], taps[1], taps[0], blank], axis=-1),
            jnp.concatenate([blank, taps[2], taps[1], taps[0]], axis=-1),
        ],
        axis=2,
    )

    blocks = pairs_all // TILE
    span = TILE * half
    work = 2 * 9 * 3 * 2 * pairs_all * half * (2 * cin) * (4 * cout)
    x_block = pl.BlockSpec((4, frames, span, 4 * cout), lambda blk, tap: (0, 0, blk, 0))
    grad_out = pl.pallas_call(
        grad_out_kernel,
        grid=(blocks, 3),
        in_specs=[
            x_block,
            pl.BlockSpec((3, 1, 2 * cin, 4 * cout), lambda blk, tap: (0, tap, 0, 0)),
            pl.BlockSpec((count * depth, mine), lambda blk, tap: (0, 0)),
        ],
        out_specs=pl.BlockSpec((frames * span, mine), lambda blk, tap: (blk, 0)),
        out_shape=jax.ShapeDtypeStruct((length, mine), jnp.bfloat16),
        scratch_shapes=[pltpu.VMEM((2, frames * span, 2 * cin), jnp.float32)],
        compiler_params=pltpu.CompilerParams(vmem_limit_bytes=LIMIT),
        cost_estimate=flops(work, 20 << 20),
        name="grad_out",
    )(shifts, big, columns)

    step = max(1, 256 // tokens_here)
    head_block = pl.BlockSpec((count, 3, tokens_here, head_dim), lambda head: (0, 0, 0, head))
    heads_here = HEADS // count
    result = pl.pallas_call(
        lambda *refs: attention_kernel(step, *refs),
        grid=(heads_here,),
        in_specs=[head_block, pl.BlockSpec((length, head_dim), lambda head: (0, head))],
        out_specs=head_block,
        out_shape=jax.ShapeDtypeStruct((count, 3, tokens_here, mine), jnp.bfloat16),
        scratch_shapes=[pltpu.VMEM((length, head_dim), jnp.float32)] * 2,
        compiler_params=pltpu.CompilerParams(vmem_limit_bytes=LIMIT),
        cost_estimate=flops(heads_here * 20 * length * length * head_dim, 8 << 20),
        name="attention",
    )(moved, grad_out)

    shifts, result = lax.optimization_barrier((shifts, result))
    back = lax.all_to_all(result, "seq", split_axis=0, concat_axis=0, tiled=True)

    scale = 1.0 / math.sqrt(frames * rows_here * count * cols)
    shards = TILE // pairs
    weight_grad = pl.pallas_call(
        lambda *refs: weight_kernel(scale, blocks, *refs),
        grid=(3, blocks),
        in_specs=[
            pl.BlockSpec(
                (shards, 2, frames, pairs * half, 2 * cin), lambda tap, blk: (blk, 0, 0, 0, 0)
            ),
            pl.BlockSpec((4, frames, span, 4 * cout), lambda tap, blk: (0, 0, blk, 0)),
        ],
        out_specs=pl.BlockSpec((3, 1, 3, cin, cout), lambda tap, blk: (0, tap, 0, 0, 0)),
        out_shape=jax.ShapeDtypeStruct((3, 3, 3, cin, cout), jnp.float32),
        scratch_shapes=[pltpu.VMEM((2, 2 * cin, frames * span), jnp.bfloat16)],
        compiler_params=pltpu.CompilerParams(vmem_limit_bytes=LIMIT),
        cost_estimate=flops(work, 20 << 20),
        name="weight_grad",
    )(feat, shifts)
    back = back.transpose(1, 2, 0, 3).reshape(3, tokens_here, inner)
    return (weight_grad, back)


def solution(mesh):
    placed = (
        P("group", "seq", None, None),
        P("group", "seq", None, None),
        P(),
        P("seq", None),
        P(None, ("group", "seq"), None),
    )
    return jax.shard_map(
        per_device,
        mesh=mesh,
        in_specs=placed,
        out_specs=(P("group", None, None, None, None), P(None, ("group", "seq"), None)),
        check_vma=False,
    )
```

profile of v0, /device:TPU:0, one launch (start us, length us, event | category | flops | bytes accessed | tf_op | source)
XLA Modules:
  0.0 260.5 jit_solution(7976161376421041125)
XLA Ops:
  7.2 0.0 all-gather.6.cloned.1.call-start
  7.2 1.2 reshape.50
  8.4 0.7 copy.39
  9.1 0.0 all-gather.6.cloned.1.call-update
  9.1 0.0 all-gather.8.cloned.1.call-start
  9.1 2.8 %reshape.55 = bf16[192,8,4,128]{3,2,1,0:T(4,128)(2,1)S(1)} reshape(bf16[192,4096]{1,0:T(8,128)(2,1)} %param.8) | data formatting | bytes 3145728 | tf_op jit(solution)/shard_map/reshape | solution.py:172
  12.0 0.8 constant_dynamic-slice_fusion
  12.8 0.2 copy.60
  13.0 25.6 %all_to_all.15 = bf16[8,192,128]{2,1,0:T(8,128)(2,1)} all-to-all(bf16[8,192,128]{2,1,0:T(8,128)(2,1)S(1)} %bitcast.59), channel_id=1, replica_groups=mesh['group'=4,'seq'=8] {'seq'}, dimensions={0} | all-to-all | bytes 786432 | tf_op jit(solution)/shard_map/all_to_all | solution.py:174
  38.5 0.0 all-gather.8.cloned.1.call-update
  38.6 3.5 %copy.42 = bf16[3,128,4096]{1,2,0:T(8,128)(2,1)S(1)} copy(bf16[3,128,4096]{2,1,0:T(8,128)(2,1)} %param.9) | data formatting | bytes 6291456 | tf_op args[4]
  42.1 2.8 %copy.43 = bf16[3,128,8,512]{3,1,0,2:T(8,128)(2,1)} copy(bf16[3,128,8,512]{1,3,2,0:T(8,128)(2,1)S(1)} %bitcast.51) | data formatting | bytes 6291456 | tf_op jit(solution)/shard_map/reshape | solution.py:166
  44.8 0.0 copy-start
  44.8 4.6 %all-to-all-start = ((bf16[8,3,128,512]{3,2,1,0:T(8,128)(2,1)}), bf16[8,3,128,512]{3,2,1,0:T(8,128)(2,1)}, u32[]{:S(2)}, u32[]{:S(2)}) async-start(bf16[8,3,128,512]{3,2,1,0:T(8,128)(2,1)} %bitcast.16), calls=%async_computation | async-start | bytes 6291456 | tf_op jit(solution)/shard_map/all_to_all | solution.py:167
  49.4 0.0 all-gather.4.cloned.1.call-start
  49.5 0.0 copy-done
  49.5 0.1 reshape.47
  49.6 0.8 copy.38
  50.4 0.0 all-gather.4.cloned.1.call-update
  50.4 4.1 %fusion = (bf16[3,3,1,384,192]{3,4,2,1,0:T(8,128)(2,1)S(1)}, bf16[3,3,1,384,192]{3,4,2,1,0:T(8,128)(2,1)}, bf16[3,3,1,384,192]{3,4,2,1,0:T(8,128)(2,1)}) fusion(bf16[3,3,3,384,192]{3,4,2,1,0:T(8,128)(2,1)} %param.7), kind=kLoop, calls=%fused_computation.12 | loop fusion | bytes 7962624 | tf_op jit(solution)/shard_map/slice | solution.py:193
  54.5 0.9 copy.53
  55.5 2.5 copy.54
  58.0 3.6 %copy.55 = bf16[3,3,1,384,192]{4,3,1,0,2:T(8,128)(2,1)} copy(bf16[3,3,1,384,192]{3,4,2,1,0:T(8,128)(2,1)} %get-tuple-element.16) | data formatting | bytes 2654208
  61.6 0.1 broadcast_in_dim.3
  61.8 12.9 %maximum_maximum_fusion.w_ref = bf16[3,3,768,768]{3,2,1,0:T(8,128)(2,1)} fusion(bf16[3,3,384,192]{3,2,1,0:T(8,128)(2,1)} %bitcast.54, bf16[3,3,384,192]{3,2,1,0:T(8,128)(2,1)S(1)} %bitcast.53, bf16[3,3,384,192]{3,2,1,0:T(8,128)(2,1)S(1)} %bitcast.52, bf16[3,3,384,192]{3,2,1,0:T(8,128)(2,1)S(1)} %broadcast_in_dim.3), kind=kLoop, calls=%fused_computation | loop fusion | flops 84934656 | bytes 15925248 | tf_op jit(solution)/shard_map/concatenate | solution.py:195
  74.7 4.9 %all-gather.6.cloned.1.call-done = bf16[2048,384]{1,0:T(8,128)(2,1)} async-done(((bf16[256,384]{1,0:T(8,128)(2,1)}), bf16[2048,384]{1,0:T(8,128)(2,1)}) %all-gather.6.cloned.1.call-update) | async-done | bytes 1572880 | tf_op jit(solution)/shard_map/all_gather | solution.py:165
  79.6 1.6 copy.40
  81.2 0.8 fusion.1
  81.9 0.7 pad_bitcast_fusion.2
  82.6 2.0 pad_maximum_fusion.1
  84.7 0.2 slice_bitcast_fusion.1
  84.9 0.1 slice.44
  85.0 0.1 slice.42
  85.1 0.1 pad_bitcast_fusion
  85.2 0.1 pad_bitcast_fusion.1
  85.3 5.8 %pad_maximum_fusion.x_ref.refs_1_ = bf16[4,4,256,768]{3,2,1,0:T(8,128)(2,1)} fusion(bf16[1,4,256,768]{3,2,1,0:T(8,128)(2,1)S(1)} %pad_bitcast_fusion, bf16[2,4,256,192]{3,2,1,0:T(8,128)(2,1)S(1)} %get-tuple-element.23, bf16[2,4,256,384]{3,2,1,0:T(8,128)(2,1)S(1)} %bitcast.48, bf16[2,4,256,192]{3,2,1,0:T(8,128)(2,1)S(1)} %get-tuple-element.26, ...), kind=kLoop, calls=%fused_computation.1 | loop fusion | flops 31457280 | bytes 12582912 | tf_op jit(solution)/shard_map/stack | solution.py:190
  91.1 24.1 %all-gather.8.cloned.1.call-done = bf16[4,1536,128]{2,1,0:T(8,128)(2,1)} async-done(((bf16[1,1536,128]{2,1,0:T(8,128)(2,1)}), bf16[4,1536,128]{2,1,0:T(8,128)(2,1)}) %all-gather.8.cloned.1.call-update) | async-done | bytes 1572880 | tf_op jit(solution)/shard_map/all_gather | solution.py:177
  115.2 2.7 %copy_bitcast_fusion.map_ref = bf16[1536,512]{1,0:T(8,128)(2,1)} fusion(bf16[4,1536,128]{2,1,0:T(8,128)(2,1)} %all-gather.8.cloned.1.call-done), kind=kLoop, calls=%fused_computation.3 | loop fusion | bytes 3145728 | tf_op jit(solution)/shard_map/reshape | solution.py:178
  118.0 30.5 %grad_out.1.refs_1_ = bf16[1024,512]{1,0:T(8,128)(2,1)} custom-call(bf16[4,4,256,768]{3,2,1,0:T(8,128)(2,1)} %pad_maximum_fusion.x_ref.refs_1_, bf16[3,3,768,768]{3,2,1,0:T(8,128)(2,1)} %maximum_maximum_fusion.w_ref, bf16[1536,512]{1,0:T(8,128)(2,1)} %copy_bitcast_fusion.map_ref), custom_call_target="tpu_custom_call" | custom-call | flops 16307453952 | bytes 20971520 | tf_op jit(solution)/shard_map/grad_out/pallas_call | solution.py:207
  148.4 0.0 all-to-all-done.refs_0_
  148.4 21.5 %attention.1 = bf16[8,3,128,512]{3,2,1,0:T(8,128)(2,1)} custom-call(bf16[8,3,128,512]{3,2,1,0:T(8,128)(2,1)} %all-to-all-done.refs_0_, bf16[1024,512]{1,0:T(8,128)(2,1)} %grad_out.1.refs_1_), custom_call_target="tpu_custom_call" | custom-call | flops 10737418240 | bytes 8388608 | tf_op jit(solution)/shard_map/attention/pallas_call | solution.py:226
  170.0 5.5 %all-to-all-start.2 = ((bf16[8,3,128,512]{3,2,1,0:T(8,128)(2,1)}), bf16[8,3,128,512]{3,2,1,0:T(8,128)(2,1)S(1)}, u32[]{:S(2)}, u32[]{:S(2)}) async-start(bf16[8,3,128,512]{3,2,1,0:T(8,128)(2,1)} %attention.1), calls=%async_computation.2 | async-start | bytes 6291456 | tf_op jit(solution)/shard_map/all_to_all | solution.py:239
  175.5 2.0 all-gather.4.cloned.1.call-done
  177.5 24.6 %weight_grad.1 = f32[3,3,3,384,192]{4,3,2,1,0:T(8,128)} custom-call(bf16[8,2,4,32,768]{4,3,2,1,0:T(8,128)(2,1)} %bitcast.62, bf16[4,4,256,768]{3,2,1,0:T(8,128)(2,1)} %pad_maximum_fusion.x_ref.refs_1_), custom_call_target="tpu_custom_call" | custom-call | flops 16307453952 | bytes 20971520 | tf_op jit(solution)/shard_map/weight_grad/pallas_call | solution.py:243
  202.0 11.6 %copy.50 = f32[3,3,3,384,192]{3,4,2,1,0:T(8,128)} copy(f32[3,3,3,384,192]{4,3,2,1,0:T(8,128)} %weight_grad.1) | data formatting | bytes 15925248
  213.7 32.9 %all-to-all-done.2 = bf16[8,3,128,512]{3,2,1,0:T(8,128)(2,1)S(1)} async-done(((bf16[8,3,128,512]{3,2,1,0:T(8,128)(2,1)}), bf16[8,3,128,512]{3,2,1,0:T(8,128)(2,1)S(1)}, u32[]{:S(2)}, u32[]{:S(2)}) %all-to-all-start.2) | async-done | bytes 3145760 | tf_op jit(solution)/shard_map/all_to_all | solution.py:239
  246.6 2.8 %copy.49 = bf16[3,128,8,512]{1,3,2,0:T(8,128)(2,1)} copy(bf16[3,128,8,512]{3,1,0,2:T(8,128)(2,1)S(1)} %bitcast.49) | data formatting | bytes 6291456 | tf_op jit(solution)/shard_map/transpose | solution.py:259
  249.4 4.6 %copy.51 = bf16[3,128,4096]{2,1,0:T(8,128)(2,1)} copy(bf16[3,128,4096]{1,2,0:T(8,128)(2,1)} %bitcast.50) | data formatting | bytes 6291456
Async XLA Ops:
  7.2 72.4 %all-gather.6.cloned.1.call-start = ((), (), s32[]{:S(2)}) async-start(), calls=%async_computation.4 | async-start | bytes 1769472 | tf_op jit(solution)/shard_map/all_gather | solution.py:165
  9.1 106.1 %all-gather.8.cloned.1.call-start = ((), (), s32[]{:S(2)}) async-start(), calls=%async_computation.5 | async-start | bytes 1966080 | tf_op jit(solution)/shard_map/all_gather | solution.py:177
  44.8 4.7 %copy-start = (bf16[4,8,16,384]{3,2,1,0:T(8,128)(2,1)S(1)}, bf16[4,8,16,384]{3,2,1,0:T(8,128)(2,1)}, u32[]{:S(2)}) copy-start(bf16[4,8,16,384]{3,2,1,0:T(8,128)(2,1)} %param.5) | copy-start | bytes 1179652
  44.8 103.6 %all-to-all-start = ((bf16[8,3,128,512]{3,2,1,0:T(8,128)(2,1)}), bf16[8,3,128,512]{3,2,1,0:T(8,128)(2,1)}, u32[]{:S(2)}, u32[]{:S(2)}) async-start(bf16[8,3,128,512]{3,2,1,0:T(8,128)(2,1)} %bitcast.16), calls=%async_computation | async-start | bytes 6291456 | tf_op jit(solution)/shard_map/all_to_all | solution.py:167
  49.4 128.0 %all-gather.4.cloned.1.call-start = ((), (), s32[]{:S(2)}) async-start(), calls=%async_computation.3 | async-start | bytes 3538944 | tf_op jit(solution)/shard_map/all_gather | solution.py:180
  170.0 76.6 %all-to-all-start.2 = ((bf16[8,3,128,512]{3,2,1,0:T(8,128)(2,1)}), bf16[8,3,128,512]{3,2,1,0:T(8,128)(2,1)S(1)}, u32[]{:S(2)}, u32[]{:S(2)}) async-start(bf16[8,3,128,512]{3,2,1,0:T(8,128)(2,1)} %attention.1), calls=%async_computation.2 | async-start | bytes 6291456 | tf_op jit(solution)/shard_map/all_to_all | solution.py:239
Sparse Core Ops, SparseCore 0:
  10.2 69.3 all-gather.5
  81.1 34.0 all-gather.7
  117.4 60.0 all-gather.3
where the time goes:
time: 262 us; the launch traced here: 261 us
  Pallas kernels  76.6 us (29%)
  waiting for transfers between devices  63.9 us (24%)
  local copies, waits for them, and re-layouts  49.5 us (19%)
  blocking collectives  25.6 us (10%)
  other arithmetic  20.7 us (8%)
  between operations  13.9 us (5%)
  starting transfers between devices  10.2 us (4%)
    all_to_all x1, waiting for transfers between devices, per_device(): lax.all_to_all(result, 'seq', split_axis=0, concat_axis=0, tiled=True)  32.9 us
    pallas_call x1, Pallas kernels, per_device(): pl.pallas_call(grad_out_kernel, grid=(blocks, 3), in_specs=[x_block, pl.B...  30.5 us
    unnamed x8, local copies, waits for them, and re-layouts  26.8 us
    all_to_all x1, blocking collectives, per_device(): lax.all_to_all(piece.transpose(1, 0, 2), 'seq', split_axis=0, concat_axis...  25.6 us
    pallas_call x1, Pallas kernels, per_device(): pl.pallas_call(lambda *refs: weight_kernel(scale, blocks, *refs), grid=(3...  24.6 us
    all_gather x1, waiting for transfers between devices, per_device(): columns = lax.all_gather(piece, 'group', axis=0, tiled=False)  24.1 us
    pallas_call x1, Pallas kernels, per_device(): pl.pallas_call(lambda *refs: attention_kernel(step, *refs), grid=(heads_h...  21.5 us
    concatenate x1, other arithmetic, per_device(): jnp.concatenate([jnp.concatenate([taps[2], taps[1], taps[0], blank], axis...  12.9 us
  transfers between devices with their start and end apart: 5, of which 4 were waited for; matrix products, arithmetic and copies ran while one was open for 23% of the time, Pallas kernels for 29%

commit v1 on v0

--- a/solution.py
+++ b/solution.py
@@ -10,6 +10,7 @@
 HEADS = 32
 TILE = 32
 LIMIT = 60 * 1024 * 1024
+MESH = pl.DeviceIdType.MESH
 
 
 def flops(count, moved):
@@ -149,7 +150,7 @@
     out_ref[:, 2] = dv_ref[...].reshape(shards, rows, width).astype(jnp.bfloat16)
 
 
-def per_device(features, cotangent, conv_weight, patch_map, qkv):
+def per_device_general(features, cotangent, conv_weight, patch_map, qkv):
     frames, rows_here, cols, cin = features.shape
     cout = cotangent.shape[3]
     count = lax.axis_size("seq")
@@ -260,6 +261,386 @@
     return (weight_grad, back)
 
 
+def fused_kernel(
+    cot_ref, feat_ref, w_ref, map_ref, qkv_ref, wout_ref, back_ref,
+    cot, feat, taps, big, cols, shifts, acc, grads, qkv_in, result, turned, dk, dv, stage,
+    cot_send, cot_recv, feat_send, feat_recv, map_send, map_recv, share_send, share_recv,
+    qkv_send, qkv_recv, back_send, back_recv, local, own, put,
+):
+    count = lax.axis_size("seq")
+    parts = lax.axis_size("group")
+    me = lax.axis_index("seq")
+    member = lax.axis_index("group")
+    lines = count // 2
+    line, side_here = me // 2, lax.rem(me, 2)
+    partner = me + 1 - 2 * side_here
+    tokens, inner = qkv_ref.shape[1], qkv_ref.shape[2]
+    mine = inner // count
+    share = mine // parts
+    depth = map_ref.shape[0]
+    heads_here, head_dim = result.shape[0], result.shape[4]
+    length = tokens * count
+    frames = cot.shape[1]
+    cin, cout = w_ref.shape[3], w_ref.shape[4]
+    span = cot.shape[2]
+    each = span // count
+
+    barrier = pltpu.get_barrier_semaphore()
+    for hop in range(1, count):
+        pl.semaphore_signal(
+            barrier, inc=1, device_id={"seq": lax.rem(me + hop, count)}, device_id_type=MESH
+        )
+    for hop in range(1, parts):
+        pl.semaphore_signal(
+            barrier, inc=1, device_id={"group": lax.rem(member + hop, parts)}, device_id_type=MESH
+        )
+    pl.semaphore_wait(barrier, count + parts - 2)
+
+    def send(src, dst, sent, got, target):
+        return pltpu.make_async_remote_copy(
+            src_ref=src, dst_ref=dst, send_sem=sent, recv_sem=got, device_id=target,
+            device_id_type=MESH,
+        )
+
+    class Gather:
+        def __init__(self, source, full, sent, got, done):
+            self.source, self.full, self.sent, self.got, self.done = source, full, sent, got, done
+
+        def rows(self, owner):
+            return self.full.at[:, :, pl.ds(pl.multiple_of(owner * each, each), each), :]
+
+        def copy(self, slot, owner, target, first=False):
+            src = self.source if first else self.rows(owner)
+            return send(
+                src, self.rows(owner), self.sent.at[slot], self.got.at[owner], {"seq": target}
+            )
+
+        def moves(self, hop):
+            if hop == 0:
+                return (
+                    (line + 1 < lines, 0, me, me + 2),
+                    (line > 0, 1, me, me - 2),
+                    (None, 2, me, partner),
+                )
+            low, high = me - 2 * hop, me + 2 * hop
+            base = 4 * hop - 1
+            has_low, has_high = line >= hop, line + hop < lines
+            return (
+                (has_low & (line + 1 < lines), base, low, me + 2),
+                (has_high & (line > 0), base + 1, high, me - 2),
+                (has_low, base + 2, low, partner),
+                (has_high, base + 3, high, partner),
+            )
+
+        def step(self, hop):
+            if hop == 0:
+                self.keep().start()
+            else:
+                for valid, owner in (
+                    (line >= hop, me - 2 * hop),
+                    (line + hop < lines, me + 2 * hop),
+                ):
+
+                    @pl.when(valid)
+                    def _():
+                        self.copy(0, owner, partner).wait_recv()
+
+            for valid, slot, owner, target in self.moves(hop):
+                copy = self.copy(slot, owner, target, first=hop == 0)
+                if valid is None:
+                    copy.start()
+                else:
+                    pl.when(valid)(copy.start)
+
+        def keep(self):
+            return pltpu.make_async_copy(self.source, self.rows(me), self.done)
+
+        def finish(self):
+            for other in range(lines):
+                self.copy(0, 2 * other + 1 - side_here, partner).wait_recv()
+            self.keep().wait()
+
+        def drain(self):
+            for hop in range(lines):
+                for valid, slot, owner, target in self.moves(hop):
+                    copy = self.copy(slot, owner, target, first=hop == 0)
+                    if valid is None:
+                        copy.wait_send()
+                    else:
+                        pl.when(valid)(copy.wait_send)
+
+    gather_cot = Gather(cot_ref, cot, cot_send, cot_recv, own.at[0])
+    gather_feat = Gather(feat_ref, feat, feat_send, feat_recv, own.at[1])
+
+    def map_piece(target):
+        return map_ref.at[:, pl.ds(pl.multiple_of(target * mine + member * share, share), share)]
+
+    def map_slot(owner):
+        return cols.at[
+            pl.ds(pl.multiple_of(owner * depth, depth), depth),
+            pl.ds(pl.multiple_of(member * share, share), share),
+        ]
+
+    def map_copy(hop):
+        target = lax.rem(me + hop, count)
+        return send(
+            map_piece(target), map_slot(me), map_send.at[hop - 1], map_recv.at[hop - 1], {"seq": target}
+        )
+
+    def share_copy(hop):
+        block = cols.at[:, pl.ds(pl.multiple_of(member * share, share), share)]
+        return send(
+            block, block, share_send.at[hop - 1], share_recv.at[hop - 1],
+            {"group": lax.rem(member + hop, parts)},
+        )
+
+    def qkv_copy(head, hop):
+        target = lax.rem(me + hop, count)
+        return send(
+            qkv_ref.at[:, :, pl.ds(pl.multiple_of(target * mine + head * head_dim, head_dim), head_dim)],
+            qkv_in.at[head, me],
+            qkv_send.at[head, hop - 1],
+            qkv_recv.at[head, hop - 1],
+            {"seq": target},
+        )
+
+    def qkv_keep(head):
+        return pltpu.make_async_copy(
+            qkv_ref.at[:, :, pl.ds(pl.multiple_of(me * mine + head * head_dim, head_dim), head_dim)],
+            qkv_in.at[head, me],
+            local.at[head],
+        )
+
+    def back_copy(head, hop):
+        target = lax.rem(me + hop, count)
+        place = back_ref.at[
+            :, :, pl.ds(pl.multiple_of(me * mine + head * head_dim, head_dim), head_dim)
+        ]
+        return send(
+            result.at[head, target], place, back_send.at[head, hop - 1],
+            back_recv.at[head, hop - 1], {"seq": target},
+        )
+
+    def back_keep(head):
+        place = back_ref.at[
+            :, :, pl.ds(pl.multiple_of(me * mine + head * head_dim, head_dim), head_dim)
+        ]
+        return pltpu.make_async_copy(result.at[head, me], place, local.at[head])
+
+    map_keep = pltpu.make_async_copy(map_piece(me), map_slot(me), own.at[2])
+    taps_in = pltpu.make_async_copy(w_ref, taps, own.at[3])
+
+    gather_cot.step(0)
+    for hop in range(1, count):
+        map_copy(hop).start()
+    taps_in.start()
+    map_keep.start()
+    for head in range(heads_here):
+        qkv_keep(head).start()
+    for hop in range(1, lines):
+        gather_cot.step(hop)
+
+    def start_head(head):
+        for hop in range(1, count):
+            qkv_copy(head, hop).start()
+
+    gather_feat.step(0)
+    start_head(0)
+    for hop in range(1, count):
+        map_copy(hop).wait_recv()
+    map_keep.wait()
+    for hop in range(1, parts):
+        share_copy(hop).start()
+
+    taps_in.wait()
+    gather_cot.finish()
+
+    row = lax.broadcasted_iota(jnp.int32, (span, 2 * cout), 0)
+    lane = lax.broadcasted_iota(jnp.int32, (span, 2 * cout), 1)
+    half = span // TILE
+    column = lax.rem(row, half)
+    ahead = (lane < cout) & (column < half - 1)
+    behind = (lane >= cout) & (column > 0)
+
+    @pl.loop(0, 2 * frames)
+    def _(index):
+        side, frame = index // frames, lax.rem(index, frames)
+        full = cot[side, frame]
+        value = full.astype(jnp.float32)
+        above = pltpu.roll(value, span - 1, 0)
+        below = pltpu.roll(value, 1, 0)
+        rest = jnp.where(ahead, above, jnp.where(behind, below, 0.0)).astype(jnp.bfloat16)
+        shifts[side + 1, frame, :, : 2 * cout] = full
+        shifts[side + 1, frame, :, 2 * cout :] = rest
+        both = jnp.concatenate([value, rest.astype(jnp.float32)], axis=1)
+        place = jnp.where(side == 0, 3, 0)
+        gap = jnp.zeros((half, 4 * cout), jnp.float32)
+        down = jnp.concatenate([gap, both[: span - half]], axis=0)
+        up = jnp.concatenate([both[half:], gap], axis=0)
+        shifts[place, frame] = jnp.where(side == 0, up, down).astype(jnp.bfloat16)
+
+    acc[...] = jnp.zeros_like(acc)
+
+    def convolve(tap_h):
+        blank = jnp.zeros((cin, cout), jnp.bfloat16)
+        for tap_t in range(3):
+            first, middle, last = (taps[tap_t, tap_h, tap_w] for tap_w in range(3))
+            big[tap_t, :cin] = jnp.concatenate([middle, first, blank, last], axis=1)
+            big[tap_t, cin:] = jnp.concatenate([last, middle, first, blank], axis=1)
+
+        @pl.loop(0, 2)
+        def _(side):
+            for tap_t in (2, 1, 0):
+                live = frames - 2 + tap_t
+                rows = shifts[side + 2 - tap_h, 2 - tap_t :].reshape(live * span, 4 * cout)
+                acc[side, : live * span] += lax.dot_general(
+                    rows, big[tap_t], (((1,), (1,)), ((), ())), preferred_element_type=jnp.float32
+                )
+
+    @pl.loop(0, 3)
+    def _(tap_h):
+        convolve(tap_h)
+        for hop in range(1, 4):
+
+            @pl.when(tap_h == hop - 1)
+            def _():
+                gather_feat.step(hop)
+                start_head(hop)
+
+    for hop in range(1, parts):
+        share_copy(hop).wait_recv()
+    total = jnp.dot(
+        acc[0].astype(jnp.bfloat16), cols[: 2 * cin], preferred_element_type=jnp.float32
+    ) + jnp.dot(acc[1].astype(jnp.bfloat16), cols[2 * cin :], preferred_element_type=jnp.float32)
+    total = total.reshape(frames, span // half, half, mine).transpose(1, 0, 2, 3)
+    total = total.reshape(length, mine).astype(jnp.bfloat16)
+    for head in range(heads_here):
+        grads[head] = total[:, head * head_dim : (head + 1) * head_dim]
+
+    step = max(1, 256 // tokens)
+
+    @pl.loop(0, heads_here)
+    def _(head):
+        qkv_keep(head).wait()
+        for hop in range(1, count):
+            qkv_copy(head, hop).wait_recv()
+        attention_kernel(step, qkv_in.at[head], grads.at[head], result.at[head], dk, dv)
+        for hop in range(1, count):
+            back_copy(head, hop).start()
+        back_keep(head).start()
+
+    gather_feat.finish()
+    for side in range(2):
+        for frame in range(frames):
+            turned[side, :, frame * span : (frame + 1) * span] = feat[side, frame].T
+
+    scale = 1.0 / math.sqrt(2 * frames * span * 2)
+
+    def out_copy(slot, tap_t, tap_h):
+        return pltpu.make_async_copy(stage.at[slot, tap_t], wout_ref.at[tap_t, tap_h], put.at[slot, tap_t])
+
+    @pl.loop(0, 3)
+    def _(tap_h):
+        slot = lax.rem(tap_h, 2)
+
+        @pl.when(tap_h == 2)
+        def _():
+            for tap_t in range(3):
+                out_copy(0, tap_t, 0).wait()
+
+        for tap_t in range(3):
+            live = frames - 2 + tap_t
+            prod = None
+            for side in range(2):
+                rows = shifts[side + 2 - tap_h, 2 - tap_t :].reshape(live * span, 4 * cout)
+                part = jnp.dot(
+                    turned[side, :, : live * span], rows, preferred_element_type=jnp.float32
+                )
+                prod = part if prod is None else prod + part
+            even, odd = prod[:cin], prod[cin:]
+            for tap_w, (low, high) in enumerate(((1, 2), (0, 1), (3, 0))):
+                value = even[:, low * cout : (low + 1) * cout] + odd[:, high * cout : (high + 1) * cout]
+                stage[slot, tap_t, tap_w] = value * scale
+            out_copy(slot, tap_t, tap_h).start()
+
+    for tap_t in range(3):
+        out_copy(1, tap_t, 1).wait()
+        out_copy(0, tap_t, 2).wait()
+
+    gather_cot.drain()
+    gather_feat.drain()
+    for hop in range(1, count):
+        map_copy(hop).wait_send()
+    for hop in range(1, parts):
+        share_copy(hop).wait_send()
+
+    @pl.loop(0, heads_here)
+    def _(head):
+        for hop in range(1, count):
+            qkv_copy(head, hop).wait_send()
+            back_copy(head, hop).wait_send()
+        for hop in range(1, count):
+            back_copy(head, hop).wait_recv()
+        back_keep(head).wait()
+
+
+def per_device(features, cotangent, conv_weight, patch_map, qkv):
+    frames, rows_here, cols, cin = features.shape
+    cout = cotangent.shape[3]
+    count, parts = lax.axis_size("seq"), lax.axis_size("group")
+    half, pairs = cols // 2, rows_here // 2
+    span = pairs * half * count
+    tokens, inner = qkv.shape[1], qkv.shape[2]
+    mine, head_dim = inner // count, inner // HEADS
+    heads_here = HEADS // count
+    depth = patch_map.shape[0]
+    fits = count == 8 and heads_here == 4 and (mine // parts) % 128 == 0
+    if not (fits and half == 8 and span == TILE * half):
+        return per_device_general(features, cotangent, conv_weight, patch_map, qkv)
+
+    def paired(value, wide):
+        value = value.reshape(frames, pairs, 2, half, 2 * wide).transpose(2, 0, 1, 3, 4)
+        return value.reshape(2, frames, pairs * half, 2 * wide)
+
+    half_type, dma = jnp.bfloat16, pltpu.SemaphoreType.DMA
+    whole = pl.BlockSpec(memory_space=pl.ANY)
+    moves = 4 * (count // 2) - 1
+    return pl.pallas_call(
+        fused_kernel,
+        in_specs=[whole] * 5,
+        out_specs=[whole] * 2,
+        out_shape=[
+            jax.ShapeDtypeStruct((3, 3, 3, cin, cout), jnp.float32),
+            jax.ShapeDtypeStruct((3, tokens, inner), half_type),
+        ],
+        scratch_shapes=[
+            pltpu.VMEM((2, frames, span, 2 * cout), half_type),
+            pltpu.VMEM((2, frames, span, 2 * cin), half_type),
+            pltpu.VMEM((3, 3, 3, cin, cout), half_type),
+            pltpu.VMEM((3, 2 * cin, 4 * cout), half_type),
+            pltpu.VMEM((count * depth, mine), half_type),
+            pltpu.VMEM((4, frames, span, 4 * cout), half_type),
+            pltpu.VMEM((2, frames * span, 2 * cin), jnp.float32),
+            pltpu.VMEM((heads_here, tokens * count, head_dim), half_type),
+            pltpu.VMEM((heads_here, count, 3, tokens, head_dim), half_type),
+            pltpu.VMEM((heads_here, count, 3, tokens, head_dim), half_type),
+            pltpu.VMEM((2, 2 * cin, frames * span), half_type),
+            pltpu.VMEM((tokens * count, head_dim), jnp.float32),
+            pltpu.VMEM((tokens * count, head_dim), jnp.float32),
+            pltpu.VMEM((2, 3, 3, cin, cout), jnp.float32),
+            dma((moves,)), dma((count,)), dma((moves,)), dma((count,)),
+            dma((count - 1,)), dma((count - 1,)), dma((parts - 1,)), dma((parts - 1,)),
+            dma((heads_here, count - 1)), dma((heads_here, count - 1)),
+            dma((heads_here, count - 1)), dma((heads_here, count - 1)),
+            dma((heads_here,)), dma((4,)), dma((2, 3)),
+        ],
+        compiler_params=pltpu.CompilerParams(
+            collective_id=0, has_side_effects=True, vmem_limit_bytes=LIMIT
+        ),
+        name="fused",
+    )(paired(cotangent, cout), paired(features, cin), conv_weight, patch_map, qkv)
+
+
 def solution(mesh):
     placed = (
         P("group", "seq", None, None),

time: 262 us -> 203 us (0.77)
  the two profiles are of different devices: /device:TPU:0 before, /device:TPU:12 now
where the time goes in v1:
time: 203 us
  Pallas kernels  177 us (87%)
  local copies, waits for them, and re-layouts  25.4 us (13%)
    pallas_call x1, Pallas kernels, per_device(): pl.pallas_call(fused_kernel, in_specs=[whole] * 5, out_specs=[whole] * 2,...  177 us
    pallas_call x1, local copies, waits for them, and re-layouts, per_device(): pl.pallas_call(fused_kernel, in_specs=[whole] * 5, out_specs=[whole] * 2,...  11.8 us
    unnamed x4, local copies, waits for them, and re-layouts  9.81 us

profile of v1, /device:TPU:12, one launch (start us, length us, event | category | flops | bytes accessed | tf_op | source)
XLA Modules:
  0.0 202.8 jit_solution(14690304708642806939)
XLA Ops:
  0.6 1.2 reshape.16
  1.8 0.7 copy.14
  2.5 1.1 reshape.18
  3.6 0.8 copy.13
  4.4 8.1 %copy.9.w_ref = bf16[3,3,3,384,192]{4,3,2,1,0:T(8,128)(2,1)} copy(bf16[3,3,3,384,192]{3,4,2,1,0:T(8,128)(2,1)} %param.7) | data formatting | bytes 7962624 | tf_op args[2]
  12.5 176.8 %fused.1 = (f32[3,3,3,384,192]{4,3,2,1,0:T(8,128)}, bf16[3,128,4096]{2,1,0:T(8,128)(2,1)}) custom-call(bf16[2,4,32,384]{3,2,1,0:T(8,128)(2,1)} %bitcast.15, bf16[2,4,32,768]{3,2,1,0:T(8,128)(2,1)} %bitcast.14, bf16[3,3,3,384,192]{4,3,2,1,0:T(8,128)(2,1)} %copy.9.w_ref, bf16[192,4096]{1,0:T(8,128)(2,1)} %map_ref.1, bf16[3,128,4096]{2,1,0:T(8,128)(2,1)} %qkv_ref.1), custom_call_target="tpu_custom_call" | custom-call | tf_op jit(solution)/shard_map/fused/pallas_call | solution.py:608
  189.3 0.0 copy-start
  189.3 11.8 %copy.10 = f32[3,3,3,384,192]{3,4,2,1,0:T(8,128)} copy(f32[3,3,3,384,192]{4,3,2,1,0:T(8,128)} %get-tuple-element.2) | data formatting | bytes 15925248 | tf_op jit(solution)/shard_map/fused/pallas_call | solution.py:608
  201.1 0.0 copy-done
  201.1 1.7 copy.16
Async XLA Ops:
  189.3 11.8 %copy-start = (bf16[3,128,4096]{2,1,0:T(8,128)(2,1)S(1)}, bf16[3,128,4096]{2,1,0:T(8,128)(2,1)}, u32[]{:S(2)}) copy-start(bf16[3,128,4096]{2,1,0:T(8,128)(2,1)} %get-tuple-element.7) | copy-start | bytes 9437188

commit v2 on v1

--- a/solution.py
+++ b/solution.py
@@ -280,10 +280,10 @@
     depth = map_ref.shape[0]
     heads_here, head_dim = result.shape[0], result.shape[4]
     length = tokens * count
-    frames = cot.shape[1]
-    cin, cout = w_ref.shape[3], w_ref.shape[4]
-    span = cot.shape[2]
-    each = span // count
+    frames, pairs_all, half = cot.shape[0], cot.shape[1], cot.shape[3]
+    cout, cin = w_ref.shape[3], w_ref.shape[4]
+    span = pairs_all * half
+    each = pairs_all // count
 
     barrier = pltpu.get_barrier_semaphore()
     for hop in range(1, count):
@@ -307,7 +307,7 @@
             self.source, self.full, self.sent, self.got, self.done = source, full, sent, got, done
 
         def rows(self, owner):
-            return self.full.at[:, :, pl.ds(pl.multiple_of(owner * each, each), each), :]
+            return self.full.at[:, pl.ds(owner * each, each)]
 
         def copy(self, slot, owner, target, first=False):
             src = self.source if first else self.rows(owner)
@@ -457,7 +457,6 @@
 
     row = lax.broadcasted_iota(jnp.int32, (span, 2 * cout), 0)
     lane = lax.broadcasted_iota(jnp.int32, (span, 2 * cout), 1)
-    half = span // TILE
     column = lax.rem(row, half)
     ahead = (lane < cout) & (column < half - 1)
     behind = (lane >= cout) & (column > 0)
@@ -465,7 +464,7 @@
     @pl.loop(0, 2 * frames)
     def _(index):
         side, frame = index // frames, lax.rem(index, frames)
-        full = cot[side, frame]
+        full = cot[frame, :, side].reshape(span, 2 * cout)
         value = full.astype(jnp.float32)
         above = pltpu.roll(value, span - 1, 0)
         below = pltpu.roll(value, 1, 0)
@@ -482,19 +481,26 @@
     acc[...] = jnp.zeros_like(acc)
 
     def convolve(tap_h):
-        blank = jnp.zeros((cin, cout), jnp.bfloat16)
+        blank = jnp.zeros((cout, cin), jnp.bfloat16)
         for tap_t in range(3):
             first, middle, last = (taps[tap_t, tap_h, tap_w] for tap_w in range(3))
-            big[tap_t, :cin] = jnp.concatenate([middle, first, blank, last], axis=1)
-            big[tap_t, cin:] = jnp.concatenate([last, middle, first, blank], axis=1)
+            for column, pieces in enumerate(
+                ((middle, first, blank, last), (last, middle, first, blank))
+            ):
+                for place, piece in enumerate(pieces):
+                    big[
+                        tap_t,
+                        place * cout : (place + 1) * cout,
+                        column * cin : (column + 1) * cin,
+                    ] = piece
 
         @pl.loop(0, 2)
         def _(side):
             for tap_t in (2, 1, 0):
                 live = frames - 2 + tap_t
                 rows = shifts[side + 2 - tap_h, 2 - tap_t :].reshape(live * span, 4 * cout)
-                acc[side, : live * span] += lax.dot_general(
-                    rows, big[tap_t], (((1,), (1,)), ((), ())), preferred_element_type=jnp.float32
+                acc[side, : live * span] += jnp.dot(
+                    rows, big[tap_t], preferred_element_type=jnp.float32
                 )
 
     @pl.loop(0, 3)
@@ -530,9 +536,11 @@
         back_keep(head).start()
 
     gather_feat.finish()
-    for side in range(2):
+
+    @pl.loop(0, 4)
+    def _(index):
         for frame in range(frames):
-            turned[side, :, frame * span : (frame + 1) * span] = feat[side, frame].T
+            turned[index, :, frame * span : (frame + 1) * span] = shifts[index, frame].T
 
     scale = 1.0 / math.sqrt(2 * frames * span * 2)
 
@@ -552,14 +560,16 @@
             live = frames - 2 + tap_t
             prod = None
             for side in range(2):
-                rows = shifts[side + 2 - tap_h, 2 - tap_t :].reshape(live * span, 4 * cout)
+                rows = feat[:live, :, side].reshape(live * span, 2 * cin)
                 part = jnp.dot(
-                    turned[side, :, : live * span], rows, preferred_element_type=jnp.float32
+                    turned[side + 2 - tap_h, :, (2 - tap_t) * span :],
+                    rows,
+                    preferred_element_type=jnp.float32,
                 )
                 prod = part if prod is None else prod + part
-            even, odd = prod[:cin], prod[cin:]
+            even, odd = prod[:, :cin], prod[:, cin:]
             for tap_w, (low, high) in enumerate(((1, 2), (0, 1), (3, 0))):
-                value = even[:, low * cout : (low + 1) * cout] + odd[:, high * cout : (high + 1) * cout]
+                value = even[low * cout : (low + 1) * cout] + odd[high * cout : (high + 1) * cout]
                 stage[slot, tap_t, tap_w] = value * scale
             out_copy(slot, tap_t, tap_h).start()
 
@@ -599,35 +609,34 @@
         return per_device_general(features, cotangent, conv_weight, patch_map, qkv)
 
     def paired(value, wide):
-        value = value.reshape(frames, pairs, 2, half, 2 * wide).transpose(2, 0, 1, 3, 4)
-        return value.reshape(2, frames, pairs * half, 2 * wide)
+        return value.reshape(frames, pairs, 2, half, 2 * wide)
 
     half_type, dma = jnp.bfloat16, pltpu.SemaphoreType.DMA
     whole = pl.BlockSpec(memory_space=pl.ANY)
     moves = 4 * (count // 2) - 1
-    return pl.pallas_call(
+    weight_grad, back = pl.pallas_call(
         fused_kernel,
         in_specs=[whole] * 5,
         out_specs=[whole] * 2,
         out_shape=[
-            jax.ShapeDtypeStruct((3, 3, 3, cin, cout), jnp.float32),
+            jax.ShapeDtypeStruct((3, 3, 3, cout, cin), jnp.float32),
             jax.ShapeDtypeStruct((3, tokens, inner), half_type),
         ],
         scratch_shapes=[
-            pltpu.VMEM((2, frames, span, 2 * cout), half_type),
-            pltpu.VMEM((2, frames, span, 2 * cin), half_type),
-            pltpu.VMEM((3, 3, 3, cin, cout), half_type),
-            pltpu.VMEM((3, 2 * cin, 4 * cout), half_type),
+            pltpu.VMEM((frames, pairs * count, 2, half, 2 * cout), half_type),
+            pltpu.VMEM((frames, pairs * count, 2, half, 2 * cin), half_type),
+            pltpu.VMEM((3, 3, 3, cout, cin), half_type),
+            pltpu.VMEM((3, 4 * cout, 2 * cin), half_type),
             pltpu.VMEM((count * depth, mine), half_type),
             pltpu.VMEM((4, frames, span, 4 * cout), half_type),
             pltpu.VMEM((2, frames * span, 2 * cin), jnp.float32),
             pltpu.VMEM((heads_here, tokens * count, head_dim), half_type),
             pltpu.VMEM((heads_here, count, 3, tokens, head_dim), half_type),
             pltpu.VMEM((heads_here, count, 3, tokens, head_dim), half_type),
-            pltpu.VMEM((2, 2 * cin, frames * span), half_type),
+            pltpu.VMEM((4, 4 * cout, frames * span), half_type),
             pltpu.VMEM((tokens * count, head_dim), jnp.float32),
             pltpu.VMEM((tokens * count, head_dim), jnp.float32),
-            pltpu.VMEM((2, 3, 3, cin, cout), jnp.float32),
+            pltpu.VMEM((2, 3, 3, cout, cin), jnp.float32),
             dma((moves,)), dma((count,)), dma((moves,)), dma((count,)),
             dma((count - 1,)), dma((count - 1,)), dma((parts - 1,)), dma((parts - 1,)),
             dma((heads_here, count - 1)), dma((heads_here, count - 1)),
@@ -638,7 +647,8 @@
             collective_id=0, has_side_effects=True, vmem_limit_bytes=LIMIT
         ),
         name="fused",
-    )(paired(cotangent, cout), paired(features, cin), conv_weight, patch_map, qkv)
+    )(paired(cotangent, cout), paired(features, cin), conv_weight.swapaxes(3, 4), patch_map, qkv)
+    return weight_grad.swapaxes(3, 4), back
 
 
 def solution(mesh):

time: 203 us -> 190 us (0.936)
  local copies, waits for them, and re-layouts: 25.4 us -> 12.9 us
    pallas_call x1 -> x0, local copies, waits for them, and re-layouts: 11.8 us -> none  [per_device(): pl.pallas_call(fused_kernel, in_specs=[whole] * 5, out_specs=[whole] * 2,...]
where the time goes in v2:
time: 190 us
  Pallas kernels  177 us (93%)
  local copies, waits for them, and re-layouts  12.9 us (7%)
    pallas_call x1, Pallas kernels, per_device(): pl.pallas_call(fused_kernel, in_specs=[whole] * 5, out_specs=[whole] * 2,...  177 us
    unnamed x4, local copies, waits for them, and re-layouts  9.18 us

profile of v2, /device:TPU:12, one launch (start us, length us, event | category | flops | bytes accessed | tf_op | source)
XLA Modules:
  0.0 190.3 jit_solution(17405666350836999086)
XLA Ops:
  0.6 1.8 reshape.10.cot_ref
  2.5 1.9 reshape.11.feat_ref
  4.3 176.7 %fused.1 = (f32[3,3,3,192,384]{4,3,2,1,0:T(8,128)}, bf16[3,128,4096]{2,1,0:T(8,128)(2,1)}) custom-call(bf16[4,4,2,8,384]{4,3,2,1,0:T(8,128)(2,1)} %reshape.10.cot_ref, bf16[4,4,2,8,768]{4,3,2,1,0:T(8,128)(2,1)} %reshape.11.feat_ref, bf16[3,3,3,192,384]{4,3,2,1,0:T(8,128)(2,1)} %bitcast.7, bf16[192,4096]{1,0:T(8,128)(2,1)} %map_ref.1, ...), custom_call_target="tpu_custom_call" | custom-call | tf_op jit(solution)/shard_map/fused/pallas_call | solution.py:617
  181.1 0.0 copy-start
  181.1 7.5 %copy.9 = f32[3,3,3,384,192]{3,4,2,1,0:T(8,128)} copy(f32[3,3,3,384,192]{3,4,2,1,0:T(8,128)} %bitcast.6) | data formatting | bytes 15925248
  188.6 0.0 copy-done
  188.6 1.7 copy.10
Async XLA Ops:
  181.1 7.5 %copy-start = (bf16[3,128,4096]{2,1,0:T(8,128)(2,1)S(1)}, bf16[3,128,4096]{2,1,0:T(8,128)(2,1)}, u32[]{:S(2)}) copy-start(bf16[3,128,4096]{2,1,0:T(8,128)(2,1)} %get-tuple-element.9) | copy-start | bytes 9437188

commit v3 on v2

--- a/solution.py
+++ b/solution.py
@@ -10,6 +10,7 @@
 HEADS = 32
 TILE = 32
 LIMIT = 60 * 1024 * 1024
+GRANT = 41 * 1024 * 1024
 MESH = pl.DeviceIdType.MESH
 
 
@@ -262,7 +263,7 @@
 
 
 def fused_kernel(
-    cot_ref, feat_ref, w_ref, map_ref, qkv_ref, wout_ref, back_ref,
+    cot_ref, feat_ref, w_ref, map_ref, qkv_ref, wout_0, wout_1, wout_2, back_ref,
     cot, feat, taps, big, cols, shifts, acc, grads, qkv_in, result, turned, dk, dv, stage,
     cot_send, cot_recv, feat_send, feat_recv, map_send, map_recv, share_send, share_recv,
     qkv_send, qkv_recv, back_send, back_recv, local, own, put,
@@ -428,12 +429,14 @@
         return pltpu.make_async_copy(result.at[head, me], place, local.at[head])
 
     map_keep = pltpu.make_async_copy(map_piece(me), map_slot(me), own.at[2])
-    taps_in = pltpu.make_async_copy(w_ref, taps, own.at[3])
+
+    def taps_in(tap_h):
+        return pltpu.make_async_copy(w_ref.at[:, tap_h], taps, own.at[3])
 
     gather_cot.step(0)
     for hop in range(1, count):
         map_copy(hop).start()
-    taps_in.start()
+    taps_in(0).start()
     map_keep.start()
     for head in range(heads_here):
         qkv_keep(head).start()
@@ -452,7 +455,6 @@
     for hop in range(1, parts):
         share_copy(hop).start()
 
-    taps_in.wait()
     gather_cot.finish()
 
     row = lax.broadcasted_iota(jnp.int32, (span, 2 * cout), 0)
@@ -481,9 +483,10 @@
     acc[...] = jnp.zeros_like(acc)
 
     def convolve(tap_h):
+        taps_in(tap_h).wait()
         blank = jnp.zeros((cout, cin), jnp.bfloat16)
         for tap_t in range(3):
-            first, middle, last = (taps[tap_t, tap_h, tap_w] for tap_w in range(3))
+            first, middle, last = (taps[tap_t, tap_w] for tap_w in range(3))
             for column, pieces in enumerate(
                 ((middle, first, blank, last), (last, middle, first, blank))
             ):
@@ -494,6 +497,10 @@
                         column * cin : (column + 1) * cin,
                     ] = piece
 
+        @pl.when(tap_h < 2)
+        def _():
+            taps_in(tap_h + 1).start()
+
         @pl.loop(0, 2)
         def _(side):
             for tap_t in (2, 1, 0):
@@ -537,24 +544,21 @@
 
     gather_feat.finish()
 
-    @pl.loop(0, 4)
-    def _(index):
-        for frame in range(frames):
-            turned[index, :, frame * span : (frame + 1) * span] = shifts[index, frame].T
-
     scale = 1.0 / math.sqrt(2 * frames * span * 2)
 
-    def out_copy(slot, tap_t, tap_h):
-        return pltpu.make_async_copy(stage.at[slot, tap_t], wout_ref.at[tap_t, tap_h], put.at[slot, tap_t])
+    def out_copy(tap_t, tap_h):
+        return pltpu.make_async_copy(
+            stage.at[tap_t], (wout_0, wout_1, wout_2)[tap_t].at[tap_h], put.at[tap_t]
+        )
 
     @pl.loop(0, 3)
     def _(tap_h):
-        slot = lax.rem(tap_h, 2)
-
-        @pl.when(tap_h == 2)
-        def _():
-            for tap_t in range(3):
-                out_copy(0, tap_t, 0).wait()
+        @pl.loop(0, 2)
+        def _(side):
+            for frame in range(frames):
+                turned[side, :, frame * span : (frame + 1) * span] = (
+                    shifts[side + 2 - tap_h, frame].T
+                )
 
         for tap_t in range(3):
             live = frames - 2 + tap_t
@@ -562,20 +566,24 @@
             for side in range(2):
                 rows = feat[:live, :, side].reshape(live * span, 2 * cin)
                 part = jnp.dot(
-                    turned[side + 2 - tap_h, :, (2 - tap_t) * span :],
+                    turned[side, :, (2 - tap_t) * span :],
                     rows,
                     preferred_element_type=jnp.float32,
                 )
                 prod = part if prod is None else prod + part
             even, odd = prod[:, :cin], prod[:, cin:]
+
+            @pl.when(tap_h > 0)
+            def _():
+                out_copy(tap_t, tap_h - 1).wait()
+
             for tap_w, (low, high) in enumerate(((1, 2), (0, 1), (3, 0))):
                 value = even[low * cout : (low + 1) * cout] + odd[high * cout : (high + 1) * cout]
-                stage[slot, tap_t, tap_w] = value * scale
-            out_copy(slot, tap_t, tap_h).start()
+                stage[tap_t, tap_w] = value * scale
+            out_copy(tap_t, tap_h).start()
 
     for tap_t in range(3):
-        out_copy(1, tap_t, 1).wait()
-        out_copy(0, tap_t, 2).wait()
+        out_copy(tap_t, 2).wait()
 
     gather_cot.drain()
     gather_feat.drain()
@@ -592,6 +600,21 @@
         for hop in range(1, count):
             back_copy(head, hop).wait_recv()
         back_keep(head).wait()
+
+
+def place_kernel(part_0, part_1, part_2, rows, weight_grad, back, done):
+    copies = [
+        pltpu.make_async_copy(part, weight_grad.at[tap], done.at[tap])
+        for tap, part in enumerate((part_0, part_1, part_2))
+    ]
+    copies += [
+        pltpu.make_async_copy(rows.at[which], back.at[which], done.at[3 + which])
+        for which in range(3)
+    ]
+    for copy in copies:
+        copy.start()
+    for copy in copies:
+        copy.wait()
 
 
 def per_device(features, cotangent, conv_weight, patch_map, qkv):
@@ -614,18 +637,18 @@
     half_type, dma = jnp.bfloat16, pltpu.SemaphoreType.DMA
     whole = pl.BlockSpec(memory_space=pl.ANY)
     moves = 4 * (count // 2) - 1
-    weight_grad, back = pl.pallas_call(
+    *weight_grad, back = pl.pallas_call(
         fused_kernel,
         in_specs=[whole] * 5,
-        out_specs=[whole] * 2,
+        out_specs=[whole] * 4,
         out_shape=[
-            jax.ShapeDtypeStruct((3, 3, 3, cout, cin), jnp.float32),
+            *[jax.ShapeDtypeStruct((3, 3, cout, cin), jnp.float32)] * 3,
             jax.ShapeDtypeStruct((3, tokens, inner), half_type),
         ],
         scratch_shapes=[
             pltpu.VMEM((frames, pairs * count, 2, half, 2 * cout), half_type),
             pltpu.VMEM((frames, pairs * count, 2, half, 2 * cin), half_type),
-            pltpu.VMEM((3, 3, 3, cout, cin), half_type),
+            pltpu.VMEM((3, 3, cout, cin), half_type),
             pltpu.VMEM((3, 4 * cout, 2 * cin), half_type),
             pltpu.VMEM((count * depth, mine), half_type),
             pltpu.VMEM((4, frames, span, 4 * cout), half_type),
@@ -633,21 +656,33 @@
             pltpu.VMEM((heads_here, tokens * count, head_dim), half_type),
             pltpu.VMEM((heads_here, count, 3, tokens, head_dim), half_type),
             pltpu.VMEM((heads_here, count, 3, tokens, head_dim), half_type),
-            pltpu.VMEM((4, 4 * cout, frames * span), half_type),
+            pltpu.VMEM((2, 4 * cout, frames * span), half_type),
             pltpu.VMEM((tokens * count, head_dim), jnp.float32),
             pltpu.VMEM((tokens * count, head_dim), jnp.float32),
-            pltpu.VMEM((2, 3, 3, cout, cin), jnp.float32),
+            pltpu.VMEM((3, 3, cout, cin), jnp.float32),
             dma((moves,)), dma((count,)), dma((moves,)), dma((count,)),
             dma((count - 1,)), dma((count - 1,)), dma((parts - 1,)), dma((parts - 1,)),
             dma((heads_here, count - 1)), dma((heads_here, count - 1)),
             dma((heads_here, count - 1)), dma((heads_here, count - 1)),
-            dma((heads_here,)), dma((4,)), dma((2, 3)),
+            dma((heads_here,)), dma((4,)), dma((3,)),
         ],
         compiler_params=pltpu.CompilerParams(
-            collective_id=0, has_side_effects=True, vmem_limit_bytes=LIMIT
+            collective_id=0, has_side_effects=True, vmem_limit_bytes=GRANT
         ),
         name="fused",
     )(paired(cotangent, cout), paired(features, cin), conv_weight.swapaxes(3, 4), patch_map, qkv)
+    weight_grad, back = pl.pallas_call(
+        place_kernel,
+        in_specs=[whole] * 4,
+        out_specs=[whole] * 2,
+        out_shape=[
+            jax.ShapeDtypeStruct((3, 3, 3, cout, cin), jnp.float32),
+            jax.ShapeDtypeStruct((3, tokens, inner), half_type),
+        ],
+        scratch_shapes=[dma((6,))],
+        compiler_params=pltpu.CompilerParams(vmem_limit_bytes=1 << 20),
+        name="place",
+    )(*weight_grad, back)
     return weight_grad.swapaxes(3, 4), back
 
 

time: 190 us -> 187 us (0.984)
  local copies, waits for them, and re-layouts: 12.9 us -> 3.7 us
  Pallas kernels: 177 us -> 182 us
    unnamed x4 -> x2, local copies, waits for them, and re-layouts: 9.18 us -> 1.4 us
    pallas_call x1 -> x2, Pallas kernels: 177 us -> 182 us  [the longest x1 178 us: per_device(): pl.pallas_call(fused_kernel, in_specs=[whole] * 5, out_specs=[whole] * 4,...]
where the time goes in v3:
time: 187 us
  Pallas kernels  182 us (97%)
  local copies, waits for them, and re-layouts  3.7 us (2%)
    pallas_call x1, Pallas kernels, per_device(): pl.pallas_call(fused_kernel, in_specs=[whole] * 5, out_specs=[whole] * 4,...  178 us
    pallas_call x1, Pallas kernels, per_device(): pl.pallas_call(place_kernel, in_specs=[whole] * 4, out_specs=[whole] * 2,...  4.2 us

profile of v3, /device:TPU:12, one launch (start us, length us, event | category | flops | bytes accessed | tf_op | source)
XLA Modules:
  0.0 186.7 jit_solution(15487497226546447377)
XLA Ops:
  0.6 1.2 reshape.10.cot_ref
  1.8 1.1 reshape.11.feat_ref
  2.9 0.0 copy-start
  2.9 1.4 copy-done
  4.3 178.0 %fused.1 = (f32[3,3,192,384]{3,2,1,0:T(8,128)S(1)}, f32[3,3,192,384]{3,2,1,0:T(8,128)S(1)}, f32[3,3,192,384]{3,2,1,0:T(8,128)S(1)}, bf16[3,128,4096]{2,1,0:T(8,128)(2,1)S(1)}) custom-call(bf16[4,4,2,8,384]{4,3,2,1,0:T(8,128)(2,1)S(1)} %reshape.10.cot_ref, bf16[4,4,2,8,768]{4,3,2,1,0:T(8,128)(2,1)S(1)} %reshape.11.feat_ref, ...), custom_call_target="tpu_custom_call" | custom-call | tf_op jit(solution)/shard_map/fused/pallas_call | solution.py:640
  182.4 4.2 %place.1 = (f32[3,3,3,192,384]{4,3,2,1,0:T(8,128)}, bf16[3,128,4096]{2,1,0:T(8,128)(2,1)}) custom-call(f32[3,3,192,384]{3,2,1,0:T(8,128)S(1)} %get-tuple-element.8.part_0, f32[3,3,192,384]{3,2,1,0:T(8,128)S(1)} %get-tuple-element.9.part_1, f32[3,3,192,384]{3,2,1,0:T(8,128)S(1)} %get-tuple-element.10.part_2, bf16[3,128,4096]{2,1,0:T(8,128)(2,1)S(1)} %get-tuple-element.11.rows), custom_call_target="tpu_custom_call" | custom-call | tf_op jit(solution)/shard_map/place/pallas_call | solution.py:674
Async XLA Ops:
  2.9 1.4 copy-start
